TPU v7x, 128 devices: a whole 4x4x4 slice. The times are simulated.
128 devices in a mesh: gx: 8 (over x, core), gy: 16 (over z, y).
Axes of the slice: x: 4, y: 4, z: 4, core: 2. Of those that a mesh axis runs over, the one named last changes fastest.
Arguments:
- parent_fields: float32 [5, 4, 384, 6144], P(None, None, 'gx', 'gy'), may hold values from -6 to 6
- parent_velocity: float32 [2, 4, 384, 6144], P(None, None, 'gx', 'gy'), may hold values from -0.3 to 0.3
- parent_mixing: float32 [4, 384, 6144], P(None, 'gx', 'gy'), may hold values from 0.01 to 0.1
- nest_fields: float32 [5, 4, 384, 6144], P(None, None, 'gx', 'gy'), may hold values from -6 to 6
- nest_velocity: float32 [2, 4, 384, 6144], P(None, None, 'gx', 'gy'), may hold values from -0.3 to 0.3
- nest_mixing: float32 [4, 384, 6144], P(None, 'gx', 'gy'), may hold values from 0.01 to 0.1
- nest_anchor: int32 [2], replicated, may hold values from 1 to 3327, as said below
Outputs:
- parent_result: float32 [5, 4, 384, 6144], P(None, None, 'gx', 'gy')
- nest_result: float32 [5, 4, 384, 6144], P(None, None, 'gx', 'gy')
Inputs may be any that keep to these rules, and one draw needn't show every extreme that they name: `nest_anchor`: the row anchor is 1 to 254; the column anchor is 3073 to 3327, so the nest with a rim of one parent cell lies inside the parent grid.
All inputs are finite; a program needn't handle non-finite values.
Results may differ from a plain program's by a relative error of at most 0.00002.
Values sent between devices are 32-bit elements; how exact they have to be, the bound alone decides.
A program may use at most 192 MiB of HBM per device.

v0:
```python
import jax
import jax.numpy as jnp
from jax import lax
from jax.sharding import PartitionSpec as P

SUBSTEPS = 3
third = 1.0 / 3.0
two_thirds = 2.0 / 3.0
nudge_floor = 0.1
relax_width = 4.0


def shift_pairs(count, step):
    return [(i, i + step) for i in range(count) if 0 <= i + step < count]


def neighbours(cells):
    rows = lax.axis_size("gx")
    cols = lax.axis_size("gy")
    western = lax.ppermute(cells[:, :, -1:, :], "gx", shift_pairs(rows, 1))
    eastern = lax.ppermute(cells[:, :, :1, :], "gx", shift_pairs(rows, -1))
    southern = lax.ppermute(cells[:, :, :, -1:], "gy", shift_pairs(cols, 1))
    northern = lax.ppermute(cells[:, :, :, :1], "gy", shift_pairs(cols, -1))
    return (western, eastern, southern, northern)


def update(values, halo, velocity, mixing):
    west_row, east_row, south_col, north_col = halo
    western = jnp.concatenate([west_row, values[:, :, :-1, :]], axis=2)
    eastern = jnp.concatenate([values[:, :, 1:, :], east_row], axis=2)
    southern = jnp.concatenate([south_col, values[:, :, :, :-1]], axis=3)
    northern = jnp.concatenate([values[:, :, :, 1:], north_col], axis=3)
    along_rows = velocity[0]
    along_columns = velocity[1]
    upwind = (
        jnp.maximum(along_rows, 0.0) * (values - western)
        + jnp.minimum(along_rows, 0.0) * (eastern - values)
        + jnp.maximum(along_columns, 0.0) * (values - southern)
        + jnp.minimum(along_columns, 0.0) * (northern - values)
    )
    return values - upwind + mixing * (eastern + western + northern + southern - 4.0 * values)


def refine_rows(block):
    lower = block[:, :, :-2]
    centre = block[:, :, 1:-1]
    upper = block[:, :, 2:]
    stacked = jnp.stack(
        (third * lower + two_thirds * centre, centre, two_thirds * centre + third * upper), axis=3
    )
    extent = centre.shape
    return stacked.reshape(extent[0], extent[1], 3 * extent[2], extent[3])


def refine_columns(block):
    lower = block[:, :, :, :-2]
    centre = block[:, :, :, 1:-1]
    upper = block[:, :, :, 2:]
    stacked = jnp.stack(
        (third * lower + two_thirds * centre, centre, two_thirds * centre + third * upper), axis=4
    )
    extent = centre.shape
    return stacked.reshape(extent[0], extent[1], extent[2], 3 * extent[3])


def grouping(count):
    rows = jnp.arange(count, dtype=jnp.int32)[:, None] // 3
    return (rows == jnp.arange(count // 3, dtype=jnp.int32)[None, :]).astype(jnp.float32)


def block_mean(state):
    extent = state.shape
    exact = lax.Precision.HIGHEST
    across = jnp.einsum("flrc,cb->flrb", state, grouping(extent[3]), precision=exact)
    down = jnp.einsum("ra,flrb->flab", grouping(extent[2]), across, precision=exact)
    return down / 9.0


def relax_weight(row_global, column_global, total_rows, total_columns):
    row_distance = jnp.minimum(row_global, total_rows - 1 - row_global)
    column_distance = jnp.minimum(column_global, total_columns - 1 - column_global)
    distance = jnp.minimum(row_distance[:, None], column_distance[None, :]).astype(jnp.float32)
    return nudge_floor + (1.0 - nudge_floor) * jnp.exp(-distance / relax_width)


def within(positions, limit):
    return (positions >= 0) & (positions < limit)


def column_pairs(count, base, ratio, k, extra):
    pairs = []
    for m in range(count):
        j = ratio * m + k
        p = base + m + extra
        if j < count and p < count:
            pairs.append((p, j))
    return pairs


def per_device(
    parent_fields,
    parent_velocity,
    parent_mixing,
    nest_fields,
    nest_velocity,
    nest_mixing,
    nest_anchor,
):
    row_rank = lax.axis_index("gx")
    column_rank = lax.axis_index("gy")
    row_devices = lax.axis_size("gx")
    column_devices = lax.axis_size("gy")
    parent_rows = parent_fields.shape[2]
    parent_columns = parent_fields.shape[3]
    nest_rows = nest_fields.shape[2]
    nest_columns = nest_fields.shape[3]
    span_rows = nest_rows // 3
    span_columns = nest_columns // 3
    ratio = parent_columns // span_columns
    base = column_devices // 2
    base_column = base * parent_columns
    relay_rows = span_rows + 2
    relay_columns = span_columns + 2
    row_anchor = nest_anchor[0]
    column_anchor = nest_anchor[1]
    offset = column_anchor - 1 - base_column
    parent_next = update(parent_fields, neighbours(parent_fields), parent_velocity, parent_mixing)
    margin = parent_columns - span_columns
    wide = jnp.pad(parent_next, ((0, 0), (0, 0), (0, 0), (margin, margin)))
    relay_cols = None
    for k in range(ratio):
        for extra in (0, 1):
            if extra == 1 and k == 0:
                continue
            start = margin + span_columns * k + offset - extra * parent_columns
            piece = lax.dynamic_slice_in_dim(wide, start, relay_columns, axis=3)
            moved = lax.ppermute(piece, "gy", column_pairs(column_devices, base, ratio, k, extra))
            relay_cols = moved if relay_cols is None else relay_cols + moved
    padded = jnp.pad(relay_cols, ((0, 0), (0, 0), (relay_rows, relay_rows), (0, 0)))
    slots = []
    for target in range(row_devices):
        first = row_anchor - 1 + span_rows * target - parent_rows * row_rank
        first = jnp.clip(first, -relay_rows, parent_rows) + relay_rows
        slots.append(lax.dynamic_slice_in_dim(padded, first, relay_rows, axis=2))
    stacked = jnp.stack(slots, axis=0)
    received = lax.all_to_all(stacked, "gx", split_axis=0, concat_axis=0, tiled=True)
    relay = jnp.sum(received, axis=0)
    forcing = refine_columns(refine_rows(relay))
    row_global = row_rank * nest_rows + jnp.arange(nest_rows, dtype=jnp.int32)
    column_global = column_rank * nest_columns + jnp.arange(nest_columns, dtype=jnp.int32)
    weight = relax_weight(
        row_global, column_global, row_devices * nest_rows, column_devices * nest_columns
    )
    state = nest_fields
    for substep in range(SUBSTEPS):
        moved = update(state, neighbours(state), nest_velocity, nest_mixing)
        state = moved + weight * (forcing - moved)
    coarse = block_mean(state)
    gathered = lax.all_gather(coarse, "gx", axis=2, tiled=True)
    total_span = row_devices * span_rows
    gathered = jnp.pad(gathered, ((0, 0), (0, 0), (parent_rows, parent_rows), (0, 0)))
    first = jnp.clip(parent_rows * row_rank - row_anchor, -parent_rows, total_span)
    strip = lax.dynamic_slice_in_dim(gathered, first + parent_rows, parent_rows, axis=2)
    pieces = []
    for extra in (1, 0):
        for k in range(ratio):
            if extra == 1 and k == 0:
                continue
            pairs = [(j, p) for p, j in column_pairs(column_devices, base, ratio, k, extra)]
            pieces.append(lax.ppermute(strip, "gy", pairs))
    joined = jnp.concatenate(pieces, axis=3)
    start = (ratio - 1) * span_columns - 1 - offset
    fed_back = lax.dynamic_slice_in_dim(joined, start, parent_columns, axis=3)
    relative_rows = row_rank * parent_rows + jnp.arange(parent_rows, dtype=jnp.int32) - row_anchor
    relative_columns = (
        column_rank * parent_columns + jnp.arange(parent_columns, dtype=jnp.int32) - column_anchor
    )
    rows_valid = within(relative_rows, total_span)
    columns_valid = within(relative_columns, column_devices * span_columns)
    covered = rows_valid[:, None] & columns_valid[None, :]
    parent_result = jnp.where(covered, fed_back, parent_next)
    return (parent_result, state)


def solution(mesh):
    placed = (
        P(None, None, "gx", "gy"),
        P(None, None, "gx", "gy"),
        P(None, "gx", "gy"),
        P(None, None, "gx", "gy"),
        P(None, None, "gx", "gy"),
        P(None, "gx", "gy"),
        P(),
    )
    return jax.shard_map(
        per_device,
        mesh=mesh,
        in_specs=placed,
        out_specs=(P(None, None, "gx", "gy"), P(None, None, "gx", "gy")),
        check_vma=False,
    )
```

profile of v0, /device:TPU:73, one launch (start us, length us, event | category | flops | bytes accessed | tf_op | source)
XLA Modules:
  0.0 324.5 jit_solution(11071260043738988761)
XLA Ops:
  11.7 3.2 collective-permute-start.6
  15.6 3.1 collective-permute-start.5
  18.7 3.0 collective-permute-start.4
  33.1 3.7 %multiply_add_fusion.3 = f32[5,4,48,384]{3,2,1,0:T(8,128)S(1)} fusion(f32[5,4,48,384]{3,2,1,0:T(8,128)S(1)} %copy-done, f32[5,4,48,1]{3,2,1,0:T(8,128)} %collective-permute-done.7, f32[5,4,48,383]{3,2,1,0:T(8,128)} %get-tuple-element.38, f32[5,4,48,383]{3,2,1,0:T(8,128)S(1)} %get-tuple-element.37, f32[5,4,48,1]{3,2,1,0:T(8,128)} %collective-permute-done.6, ...), kind=kLoop, calls=%fused_computation.35 | loop fusion | flops 8478720 | bytes 10321920 | tf_op jit(solution)/shard_map/add | solution.py:41
  36.8 2.9 pad_dynamic-slice_fusion.3
  39.8 3.3 %collective-permute-start.12 = (f32[5,4,48,130]{3,2,1,0:T(8,128)}, f32[5,4,48,130]{3,2,1,0:T(8,128)}, u32[]{:S(2)}, u32[]{:S(2)}) collective-permute-start(f32[5,4,48,130]{3,2,1,0:T(8,128)} %get-tuple-element.29), channel_id=1, source_target_pairs={{9,2},{10,5},{11,8},{12,11},{13,14},{25,18},{26,21},{27,24},{28,27... | collective-permute-start | bytes 1497608 | tf_op jit(solution)/shard_map/ppermute | solution.py:137
  58.9 25.7 %collective-permute-done.12 = f32[5,4,48,130]{3,2,1,0:T(8,128)} collective-permute-done((f32[5,4,48,130]{3,2,1,0:T(8,128)}, f32[5,4,48,130]{3,2,1,0:T(8,128)}, u32[]{:S(2)}, u32[]{:S(2)}) %collective-permute-start.12) | collective-permute-done | bytes 499232 | tf_op jit(solution)/shard_map/ppermute | solution.py:137
  84.6 28.6 %collective-permute-start.3 = (f32[5,4,48,1]{3,2,1,0:T(8,128)}, f32[5,4,48,1]{3,2,1,0:T(8,128)}, u32[]{:S(2)}, u32[]{:S(2)}) collective-permute-start(f32[5,4,48,1]{3,2,1,0:T(8,128)} %get-tuple-element.23), channel_id=1, source_target_pairs={{1,0},{2,1},{3,2},{4,3},{5,4},{6,5},{7,6},{8,7},{9,8},{10,9},{11,1... | collective-permute-start | bytes 11528 | tf_op jit(solution)/shard_map/ppermute | solution.py:23
  117.9 2.8 collective-permute-start
  131.5 4.6 %all-to-all-start = ((f32[8,5,4,18,130]{4,2,3,1,0:T(4,128)}), f32[8,5,4,18,130]{4,2,3,1,0:T(4,128)}, u32[]{:S(2)}, u32[]{:S(2)}) async-start(f32[8,5,4,18,130]{4,2,3,1,0:T(4,128)} %bitcast_dynamic-update-slice_fusion), calls=%async_computation | async-start | bytes 5898240 | tf_op jit(solution)/shard_map/all_to_all | solution.py:146
  142.0 29.8 %all-to-all-done = f32[8,5,4,18,130]{4,2,3,1,0:T(4,128)} async-done(((f32[8,5,4,18,130]{4,2,3,1,0:T(4,128)}), f32[8,5,4,18,130]{4,2,3,1,0:T(4,128)}, u32[]{:S(2)}, u32[]{:S(2)}) %all-to-all-start) | async-done | bytes 1497632 | tf_op jit(solution)/shard_map/all_to_all | solution.py:146
  176.3 3.6 %copy.41 = f32[5,4,48,128,3]{2,1,4,3,0:T(4,128)} copy(f32[5,4,48,128,3]{3,1,2,0,4:T(4,128)S(1)} %pad_maximum_fusion.8) | data formatting | bytes 2949120 | tf_op jit(solution)/shard_map/stack | solution.py:59
  179.9 3.4 %copy.42 = f32[5,4,48,384]{3,2,1,0:T(8,128)S(1)} copy(f32[5,4,48,384]{2,1,3,0:T(4,128)} %bitcast.62) | data formatting | bytes 2949120 | tf_op jit(solution)/shard_map/reshape | solution.py:63
  183.3 4.1 %multiply_add_fusion.2 = f32[5,4,48,384]{3,2,1,0:T(8,128)S(1)} fusion(f32[5,4,48,384]{3,2,1,0:T(8,128)S(1)} %copy.42, f32[5,4,48,384]{3,2,1,0:T(8,128)S(1)} %copy-done.1, f32[5,4,48,1]{3,2,1,0:T(8,128)} %collective-permute-done.3, f32[5,4,48,383]{3,2,1,0:T(8,128)} %get-tuple-element.25, f32[5,4,48,383]{3,2,1,0:T(8,128)} %get-tuple-element.24, ...), kind=kLoop, calls=%fused_computation.34 | loop fusion | flops 9584640 | bytes 11870208 | tf_op jit(solution)/shard_map/add | solution.py:157
  188.2 3.6 %collective-permute-start.16 = (f32[5,4,48,1]{3,2,1,0:T(8,128)S(1)}, f32[5,4,48,1]{3,2,1,0:T(8,128)S(1)}, u32[]{:S(2)}, u32[]{:S(2)}) collective-permute-start(f32[5,4,48,1]{3,2,1,0:T(8,128)S(1)} %get-tuple-element.15), channel_id=1, source_target_pairs={{1,0},{2,1},{3,2},{4,3},{5,4},{6,5},{7,6},{8,7},{9,8},{10,9},{11,1... | collective-permute-start | bytes 11528 | tf_op jit(solution)/shard_map/ppermute | solution.py:23
  193.8 3.1 collective-permute-start.14
  202.0 4.7 %collective-permute-done.15 = f32[5,4,48,1]{3,2,1,0:T(8,128)S(1)} collective-permute-done((f32[5,4,48,1]{3,2,1,0:T(8,128)S(1)}, f32[5,4,48,1]{3,2,1,0:T(8,128)S(1)}, u32[]{:S(2)}, u32[]{:S(2)}) %collective-permute-start.15) | collective-permute-done | bytes 3872 | tf_op jit(solution)/shard_map/ppermute | solution.py:22
  209.2 5.2 %collective-permute-start.20 = (f32[5,4,48,1]{3,2,1,0:T(8,128)S(1)}, f32[5,4,48,1]{3,2,1,0:T(8,128)S(1)}, u32[]{:S(2)}, u32[]{:S(2)}) collective-permute-start(f32[5,4,48,1]{3,2,1,0:T(8,128)S(1)} %get-tuple-element.7), channel_id=1, source_target_pairs={{1,0},{2,1},{3,2},{4,3},{5,4},{6,5},{7,6},{8,7},{9,8},{10,9},{11,1... | collective-permute-start | bytes 11528 | tf_op jit(solution)/shard_map/ppermute | solution.py:23
  216.4 4.3 %collective-permute-start.18 = (f32[5,4,1,384]{3,2,1,0:T(1,128)S(1)}, f32[5,4,1,384]{3,2,1,0:T(1,128)S(1)}, u32[]{:S(2)}, u32[]{:S(2)}) collective-permute-start(f32[5,4,1,384]{3,2,1,0:T(1,128)S(1)} %get-tuple-element.3), channel_id=1, source_target_pairs={{16,0},{32,16},{48,32},{64,48},{80,64},{96,80},{112,96},{17,1},{33... | collective-permute-start | bytes 92168 | tf_op jit(solution)/shard_map/ppermute | solution.py:21
  223.0 3.7 %collective-permute-done.19 = f32[5,4,48,1]{3,2,1,0:T(8,128)S(1)} collective-permute-done((f32[5,4,48,1]{3,2,1,0:T(8,128)S(1)}, f32[5,4,48,1]{3,2,1,0:T(8,128)S(1)}, u32[]{:S(2)}, u32[]{:S(2)}) %collective-permute-start.19) | collective-permute-done | bytes 3872 | tf_op jit(solution)/shard_map/ppermute | solution.py:22
  230.9 25.4 %all-gather.2.cloned.1.call-done = f32[5,4,128,128]{3,2,1,0:T(8,128)} async-done(((f32[5,4,16,128]{3,2,1,0:T(8,128)}), f32[5,4,128,128]{3,2,1,0:T(8,128)}) %all-gather.2.cloned.1.call-update) | async-done | bytes 1310736 | tf_op jit(solution)/shard_map/all_gather | solution.py:159
  260.5 5.3 %collective-permute-start.23 = (f32[5,4,48,128]{3,2,1,0:T(8,128)S(1)}, f32[5,4,48,128]{3,2,1,0:T(8,128)S(1)}, u32[]{:S(2)}, u32[]{:S(2)}) collective-permute-start(f32[5,4,48,128]{3,2,1,0:T(8,128)S(1)} %pad_dynamic-slice_fusion.13), channel_id=1, source_target_pairs={{0,8},{3,9},{6,10},{9,11},{12,12},{15,13},{16,24},{19,25},{22,26},... | collective-permute-start | bytes 1474568 | tf_op jit(solution)/shard_map/ppermute | solution.py:170
  269.1 35.8 %collective-permute-done.21 = f32[5,4,48,128]{3,2,1,0:T(8,128)S(1)} collective-permute-done((f32[5,4,48,128]{3,2,1,0:T(8,128)S(1)}, f32[5,4,48,128]{3,2,1,0:T(8,128)S(1)}, u32[]{:S(2)}, u32[]{:S(2)}) %collective-permute-start.21) | collective-permute-done | bytes 491552 | tf_op jit(solution)/shard_map/ppermute | solution.py:170
  305.1 10.8 %collective-permute-done.25 = f32[5,4,48,128]{3,2,1,0:T(8,128)S(1)} collective-permute-done((f32[5,4,48,128]{3,2,1,0:T(8,128)S(1)}, f32[5,4,48,128]{3,2,1,0:T(8,128)S(1)}, u32[]{:S(2)}, u32[]{:S(2)}) %collective-permute-start.25) | collective-permute-done | bytes 491552 | tf_op jit(solution)/shard_map/ppermute | solution.py:170
  (117 shorter events, 74.0 us)
Async XLA Ops:
  9.6 23.5 %collective-permute-start.7 = (f32[5,4,48,1]{3,2,1,0:T(8,128)}, f32[5,4,48,1]{3,2,1,0:T(8,128)}, u32[]{:S(2)}, u32[]{:S(2)}) collective-permute-start(f32[5,4,48,1]{3,2,1,0:T(8,128)} %get-tuple-element.36), channel_id=1, source_target_pairs={{1,0},{2,1},{3,2},{4,3},{5,4},{6,5},{7,6},{8,7},{9,8},{10,9},{11,1... | collective-permute-start | bytes 11528 | tf_op jit(solution)/shard_map/ppermute | solution.py:23
  11.7 21.4 %collective-permute-start.6 = (f32[5,4,48,1]{3,2,1,0:T(8,128)}, f32[5,4,48,1]{3,2,1,0:T(8,128)}, u32[]{:S(2)}, u32[]{:S(2)}) collective-permute-start(f32[5,4,48,1]{3,2,1,0:T(8,128)} %get-tuple-element.35), channel_id=1, source_target_pairs={{0,1},{1,2},{2,3},{3,4},{4,5},{5,6},{6,7},{7,8},{8,9},{9,10},{10,1... | collective-permute-start | bytes 11528 | tf_op jit(solution)/shard_map/ppermute | solution.py:22
  15.6 17.5 %collective-permute-start.5 = (f32[5,4,1,384]{3,2,1,0:T(1,128)}, f32[5,4,1,384]{3,2,1,0:T(1,128)}, u32[]{:S(2)}, u32[]{:S(2)}) collective-permute-start(f32[5,4,1,384]{3,2,1,0:T(1,128)} %get-tuple-element.32), channel_id=1, source_target_pairs={{16,0},{32,16},{48,32},{64,48},{80,64},{96,80},{112,96},{17,1},{33... | collective-permute-start | bytes 92168 | tf_op jit(solution)/shard_map/ppermute | solution.py:21
  18.7 14.4 %collective-permute-start.4 = (f32[5,4,1,384]{3,2,1,0:T(1,128)}, f32[5,4,1,384]{3,2,1,0:T(1,128)}, u32[]{:S(2)}, u32[]{:S(2)}) collective-permute-start(f32[5,4,1,384]{3,2,1,0:T(1,128)} %get-tuple-element.31), channel_id=1, source_target_pairs={{0,16},{16,32},{32,48},{48,64},{64,80},{80,96},{96,112},{1,17},{17... | collective-permute-start | bytes 92168 | tf_op jit(solution)/shard_map/ppermute | solution.py:20
  39.8 44.8 %collective-permute-start.12 = (f32[5,4,48,130]{3,2,1,0:T(8,128)}, f32[5,4,48,130]{3,2,1,0:T(8,128)}, u32[]{:S(2)}, u32[]{:S(2)}) collective-permute-start(f32[5,4,48,130]{3,2,1,0:T(8,128)} %get-tuple-element.29), channel_id=1, source_target_pairs={{9,2},{10,5},{11,8},{12,11},{13,14},{25,18},{26,21},{27,24},{28,27... | collective-permute-start | bytes 1497608 | tf_op jit(solution)/shard_map/ppermute | solution.py:137
  43.0 70.1 %collective-permute-start.11 = (f32[5,4,48,130]{3,2,1,0:T(8,128)}, f32[5,4,48,130]{3,2,1,0:T(8,128)}, u32[]{:S(2)}, u32[]{:S(2)}) collective-permute-start(f32[5,4,48,130]{3,2,1,0:T(8,128)} %get-tuple-element.28), channel_id=1, source_target_pairs={{8,2},{9,5},{10,8},{11,11},{12,14},{24,18},{25,21},{26,24},{27,27}... | collective-permute-start | bytes 1497608 | tf_op jit(solution)/shard_map/ppermute | solution.py:137
  45.3 69.8 %collective-permute-start.10 = (f32[5,4,48,130]{3,2,1,0:T(8,128)}, f32[5,4,48,130]{3,2,1,0:T(8,128)}, u32[]{:S(2)}, u32[]{:S(2)}) collective-permute-start(f32[5,4,48,130]{3,2,1,0:T(8,128)} %get-tuple-element.27), channel_id=1, source_target_pairs={{9,1},{10,4},{11,7},{12,10},{13,13},{25,17},{26,20},{27,23},{28,26... | collective-permute-start | bytes 1497608 | tf_op jit(solution)/shard_map/ppermute | solution.py:137
  47.5 70.3 %collective-permute-start.8 = (f32[5,4,48,130]{3,2,1,0:T(8,128)S(1)}, f32[5,4,48,130]{3,2,1,0:T(8,128)}, u32[]{:S(2)}, u32[]{:S(2)}) collective-permute-start(f32[5,4,48,130]{3,2,1,0:T(8,128)S(1)} %get-tuple-element.30), channel_id=1, source_target_pairs={{8,0},{9,3},{10,6},{11,9},{12,12},{13,15},{24,16},{25,19},{26,22},... | collective-permute-start | bytes 1497608 | tf_op jit(solution)/shard_map/ppermute | solution.py:137
  49.8 71.0 %collective-permute-start.9 = (f32[5,4,48,130]{3,2,1,0:T(8,128)S(1)}, f32[5,4,48,130]{3,2,1,0:T(8,128)}, u32[]{:S(2)}, u32[]{:S(2)}) collective-permute-start(f32[5,4,48,130]{3,2,1,0:T(8,128)S(1)} %get-tuple-element.26), channel_id=1, source_target_pairs={{8,1},{9,4},{10,7},{11,10},{12,13},{24,17},{25,20},{26,23},{27,26}... | collective-permute-start | bytes 1497608 | tf_op jit(solution)/shard_map/ppermute | solution.py:137
  84.6 98.7 %collective-permute-start.3 = (f32[5,4,48,1]{3,2,1,0:T(8,128)}, f32[5,4,48,1]{3,2,1,0:T(8,128)}, u32[]{:S(2)}, u32[]{:S(2)}) collective-permute-start(f32[5,4,48,1]{3,2,1,0:T(8,128)} %get-tuple-element.23), channel_id=1, source_target_pairs={{1,0},{2,1},{3,2},{4,3},{5,4},{6,5},{7,6},{8,7},{9,8},{10,9},{11,1... | collective-permute-start | bytes 11528 | tf_op jit(solution)/shard_map/ppermute | solution.py:23
  113.2 70.1 %collective-permute-start.2 = (f32[5,4,48,1]{3,2,1,0:T(8,128)}, f32[5,4,48,1]{3,2,1,0:T(8,128)}, u32[]{:S(2)}, u32[]{:S(2)}) collective-permute-start(f32[5,4,48,1]{3,2,1,0:T(8,128)} %get-tuple-element.22), channel_id=1, source_target_pairs={{0,1},{1,2},{2,3},{3,4},{4,5},{5,6},{6,7},{7,8},{8,9},{9,10},{10,1... | collective-permute-start | bytes 11528 | tf_op jit(solution)/shard_map/ppermute | solution.py:22
  115.1 68.2 %collective-permute-start.1 = (f32[5,4,1,384]{3,2,1,0:T(1,128)}, f32[5,4,1,384]{3,2,1,0:T(1,128)}, u32[]{:S(2)}, u32[]{:S(2)}) collective-permute-start(f32[5,4,1,384]{3,2,1,0:T(1,128)} %get-tuple-element.19), channel_id=1, source_target_pairs={{16,0},{32,16},{48,32},{64,48},{80,64},{96,80},{112,96},{17,1},{33... | collective-permute-start | bytes 92168 | tf_op jit(solution)/shard_map/ppermute | solution.py:21
  117.9 65.4 %collective-permute-start = (f32[5,4,1,384]{3,2,1,0:T(1,128)}, f32[5,4,1,384]{3,2,1,0:T(1,128)}, u32[]{:S(2)}, u32[]{:S(2)}) collective-permute-start(f32[5,4,1,384]{3,2,1,0:T(1,128)} %get-tuple-element.18), channel_id=1, source_target_pairs={{0,16},{16,32},{32,48},{48,64},{64,80},{80,96},{96,112},{1,17},{17... | collective-permute-start | bytes 92168 | tf_op jit(solution)/shard_map/ppermute | solution.py:20
  131.5 40.2 %all-to-all-start = ((f32[8,5,4,18,130]{4,2,3,1,0:T(4,128)}), f32[8,5,4,18,130]{4,2,3,1,0:T(4,128)}, u32[]{:S(2)}, u32[]{:S(2)}) async-start(f32[8,5,4,18,130]{4,2,3,1,0:T(4,128)} %bitcast_dynamic-update-slice_fusion), calls=%async_computation | async-start | bytes 5898240 | tf_op jit(solution)/shard_map/all_to_all | solution.py:146
  136.2 120.2 %all-gather.2.cloned.1.call-start = ((), (), s32[]{:S(2)}) async-start(), calls=%async_computation.1 | async-start | bytes 1474560 | tf_op jit(solution)/shard_map/all_gather | solution.py:159
  188.2 13.8 %collective-permute-start.16 = (f32[5,4,48,1]{3,2,1,0:T(8,128)S(1)}, f32[5,4,48,1]{3,2,1,0:T(8,128)S(1)}, u32[]{:S(2)}, u32[]{:S(2)}) collective-permute-start(f32[5,4,48,1]{3,2,1,0:T(8,128)S(1)} %get-tuple-element.15), channel_id=1, source_target_pairs={{1,0},{2,1},{3,2},{4,3},{5,4},{6,5},{7,6},{8,7},{9,8},{10,9},{11,1... | collective-permute-start | bytes 11528 | tf_op jit(solution)/shard_map/ppermute | solution.py:23
  191.9 14.8 %collective-permute-start.15 = (f32[5,4,48,1]{3,2,1,0:T(8,128)S(1)}, f32[5,4,48,1]{3,2,1,0:T(8,128)S(1)}, u32[]{:S(2)}, u32[]{:S(2)}) collective-permute-start(f32[5,4,48,1]{3,2,1,0:T(8,128)S(1)} %get-tuple-element.14), channel_id=1, source_target_pairs={{0,1},{1,2},{2,3},{3,4},{4,5},{5,6},{6,7},{7,8},{8,9},{9,10},{10,1... | collective-permute-start | bytes 11528 | tf_op jit(solution)/shard_map/ppermute | solution.py:22
  193.8 12.9 %collective-permute-start.14 = (f32[5,4,1,384]{3,2,1,0:T(1,128)S(1)}, f32[5,4,1,384]{3,2,1,0:T(1,128)S(1)}, u32[]{:S(2)}, u32[]{:S(2)}) collective-permute-start(f32[5,4,1,384]{3,2,1,0:T(1,128)S(1)} %get-tuple-element.11), channel_id=1, source_target_pairs={{16,0},{32,16},{48,32},{64,48},{80,64},{96,80},{112,96},{17,1},{33... | collective-permute-start | bytes 92168 | tf_op jit(solution)/shard_map/ppermute | solution.py:21
  209.2 13.7 %collective-permute-start.20 = (f32[5,4,48,1]{3,2,1,0:T(8,128)S(1)}, f32[5,4,48,1]{3,2,1,0:T(8,128)S(1)}, u32[]{:S(2)}, u32[]{:S(2)}) collective-permute-start(f32[5,4,48,1]{3,2,1,0:T(8,128)S(1)} %get-tuple-element.7), channel_id=1, source_target_pairs={{1,0},{2,1},{3,2},{4,3},{5,4},{6,5},{7,6},{8,7},{9,8},{10,9},{11,1... | collective-permute-start | bytes 11528 | tf_op jit(solution)/shard_map/ppermute | solution.py:23
  257.3 47.6 %collective-permute-start.21 = (f32[5,4,48,128]{3,2,1,0:T(8,128)S(1)}, f32[5,4,48,128]{3,2,1,0:T(8,128)S(1)}, u32[]{:S(2)}, u32[]{:S(2)}) collective-permute-start(f32[5,4,48,128]{3,2,1,0:T(8,128)S(1)} %pad_dynamic-slice_fusion.13), channel_id=1, source_target_pairs={{1,9},{4,10},{7,11},{10,12},{13,13},{17,25},{20,26},{23,27},{26,28... | collective-permute-start | bytes 1474568 | tf_op jit(solution)/shard_map/ppermute | solution.py:170
  258.6 46.4 %collective-permute-start.22 = (f32[5,4,48,128]{3,2,1,0:T(8,128)S(1)}, f32[5,4,48,128]{3,2,1,0:T(8,128)S(1)}, u32[]{:S(2)}, u32[]{:S(2)}) collective-permute-start(f32[5,4,48,128]{3,2,1,0:T(8,128)S(1)} %pad_dynamic-slice_fusion.13), channel_id=1, source_target_pairs={{2,9},{5,10},{8,11},{11,12},{14,13},{18,25},{21,26},{24,27},{27,28... | collective-permute-start | bytes 1474568 | tf_op jit(solution)/shard_map/ppermute | solution.py:170
  260.5 44.5 %collective-permute-start.23 = (f32[5,4,48,128]{3,2,1,0:T(8,128)S(1)}, f32[5,4,48,128]{3,2,1,0:T(8,128)S(1)}, u32[]{:S(2)}, u32[]{:S(2)}) collective-permute-start(f32[5,4,48,128]{3,2,1,0:T(8,128)S(1)} %pad_dynamic-slice_fusion.13), channel_id=1, source_target_pairs={{0,8},{3,9},{6,10},{9,11},{12,12},{15,13},{16,24},{19,25},{22,26},... | collective-permute-start | bytes 1474568 | tf_op jit(solution)/shard_map/ppermute | solution.py:170
  266.4 38.6 %collective-permute-start.24 = (f32[5,4,48,128]{3,2,1,0:T(8,128)S(1)}, f32[5,4,48,128]{3,2,1,0:T(8,128)S(1)}, u32[]{:S(2)}, u32[]{:S(2)}) collective-permute-start(f32[5,4,48,128]{3,2,1,0:T(8,128)S(1)} %pad_dynamic-slice_fusion.13), channel_id=1, source_target_pairs={{1,8},{4,9},{7,10},{10,11},{13,12},{17,24},{20,25},{23,26},{26,27}... | collective-permute-start | bytes 1474568 | tf_op jit(solution)/shard_map/ppermute | solution.py:170
  267.8 48.1 %collective-permute-start.25 = (f32[5,4,48,128]{3,2,1,0:T(8,128)S(1)}, f32[5,4,48,128]{3,2,1,0:T(8,128)S(1)}, u32[]{:S(2)}, u32[]{:S(2)}) collective-permute-start(f32[5,4,48,128]{3,2,1,0:T(8,128)S(1)} %pad_dynamic-slice_fusion.13), channel_id=1, source_target_pairs={{2,8},{5,9},{8,10},{11,11},{14,12},{18,24},{21,25},{24,26},{27,27}... | collective-permute-start | bytes 1474568 | tf_op jit(solution)/shard_map/ppermute | solution.py:170
  (16 other events, 156.7 us)
Sparse Core Ops, SparseCore 0:
  230.4 25.9 all-gather.1
where the time goes:
time: 326 us; the launch traced here: 324 us
  waiting for transfers between devices  138 us (42%)
  starting transfers between devices  99.6 us (31%)
  local copies, waits for them, and re-layouts  34.8 us (11%)
  between operations  26.7 us (8%)
  other arithmetic  23.4 us (7%)
    ppermute x5, waiting for transfers between devices, per_device(): pieces.append(lax.ppermute(strip, 'gy', pairs))  46.6 us
    ppermute x4, starting transfers between devices, neighbours(): northern = lax.ppermute(cells[:, :, :, :1], 'gy', shift_pairs(cols, -1))  39.5 us
    all_to_all x1, waiting for transfers between devices, per_device(): lax.all_to_all(stacked, 'gx', split_axis=0, concat_axis=0, tiled=True)  29.8 us
    ppermute x5, waiting for transfers between devices, per_device(): lax.ppermute(piece, 'gy', column_pairs(column_devices, base, ratio, k, ex...  25.7 us
    all_gather x1, waiting for transfers between devices, per_device(): gathered = lax.all_gather(coarse, 'gx', axis=2, tiled=True)  25.4 us
    ppermute x4, starting transfers between devices, neighbours(): eastern = lax.ppermute(cells[:, :, :1, :], 'gx', shift_pairs(rows, -1))  13.2 us
    ppermute x5, starting transfers between devices, per_device(): lax.ppermute(piece, 'gy', column_pairs(column_devices, base, ratio, k, ex...  12.3 us
    ppermute x4, starting transfers between devices, neighbours(): western = lax.ppermute(cells[:, :, -1:, :], 'gx', shift_pairs(rows, 1))  10.6 us
  transfers between devices with their start and end apart: 28, of which 8 were waited for; matrix products, arithmetic and copies ran while one was open for 12% of the time, Pallas kernels for 0%

commit v1 on v0

--- a/solution.py
+++ b/solution.py
@@ -156,7 +156,18 @@
         moved = update(state, neighbours(state), nest_velocity, nest_mixing)
         state = moved + weight * (forcing - moved)
     coarse = block_mean(state)
-    gathered = lax.all_gather(coarse, "gx", axis=2, tiled=True)
+    axis_total = lax.axis_size("gx")
+    by_rank = [(d, (d + 1) % axis_total) for d in range(axis_total)]
+    entries = [(d, (d - 1) % axis_total) for d in range(axis_total)]
+    r1, f_now = ([coarse], [coarse])
+    for _ in range(axis_total // 2):
+        r1.append(lax.ppermute(r1[-1], axis_name="gx", perm=by_rank))
+    ii = 0
+    while ii < (axis_total - 1) // 2:
+        f_now.append(lax.ppermute(f_now[-1], axis_name="gx", perm=entries))
+        ii += 1
+    val2 = jnp.concatenate([*r1[::-1], *f_now[1:]], axis=2)
+    gathered = jnp.roll(val2, (lax.axis_index("gx") - axis_total // 2) * coarse.shape[2], axis=2)
     total_span = row_devices * span_rows
     gathered = jnp.pad(gathered, ((0, 0), (0, 0), (parent_rows, parent_rows), (0, 0)))
     first = jnp.clip(parent_rows * row_rank - row_anchor, -parent_rows, total_span)

time: 326 us -> 309 us (0.948)
  waiting for transfers between devices: 138 us -> 118 us
  starting transfers between devices: 99.6 us -> 117 us
  between operations: 26.7 us -> 13 us
    all_gather x1 -> x0, waiting for transfers between devices: 25.4 us -> none  [per_device(): gathered = lax.all_gather(coarse, 'gx', axis=2, tiled=True)]
    ppermute x0 -> x7, starting transfers between devices: none -> 16.5 us  [the longest x4 10 us: per_device(): r1.append(lax.ppermute(r1[-1], axis_name='gx', perm=by_rank))]
    ppermute x0 -> x7, waiting for transfers between devices: none -> 5.78 us  [the longest x4 4.63 us: per_device(): r1.append(lax.ppermute(r1[-1], axis_name='gx', perm=by_rank))]
    unnamed x35 -> x50, local copies, waits for them, and re-layouts: 6.43 us -> 6.69 us
  transfers between devices with their start and end apart: 28 -> 34, of which waited for: 8 -> 13; matrix products, arithmetic and copies ran while one was open for 12% -> 12% of each run, Pallas kernels for 0% -> 0%
where the time goes in v1:
time: 309 us; the launch traced here: 307 us
  waiting for transfers between devices  118 us (38%)
  starting transfers between devices  117 us (38%)
  local copies, waits for them, and re-layouts  34.3 us (11%)
  other arithmetic  23.3 us (8%)
  between operations  13 us (4%)
    ppermute x5, waiting for transfers between devices, per_device(): pieces.append(lax.ppermute(strip, 'gy', pairs))  45.7 us
    ppermute x4, starting transfers between devices, neighbours(): northern = lax.ppermute(cells[:, :, :, :1], 'gy', shift_pairs(cols, -1))  39.4 us
    all_to_all x1, waiting for transfers between devices, per_device(): lax.all_to_all(stacked, 'gx', split_axis=0, concat_axis=0, tiled=True)  29.8 us
    ppermute x5, waiting for transfers between devices, per_device(): lax.ppermute(piece, 'gy', column_pairs(column_devices, base, ratio, k, ex...  26.2 us
    ppermute x4, starting transfers between devices, neighbours(): eastern = lax.ppermute(cells[:, :, :1, :], 'gx', shift_pairs(rows, -1))  13.2 us
    ppermute x5, starting transfers between devices, per_device(): lax.ppermute(piece, 'gy', column_pairs(column_devices, base, ratio, k, ex...  12.3 us
    ppermute x5, starting transfers between devices, per_device(): pieces.append(lax.ppermute(strip, 'gy', pairs))  11.4 us
    ppermute x4, starting transfers between devices, neighbours(): western = lax.ppermute(cells[:, :, -1:, :], 'gx', shift_pairs(rows, 1))  10.6 us
  transfers between devices with their start and end apart: 34, of which 13 were waited for; matrix products, arithmetic and copies ran while one was open for 12% of the time, Pallas kernels for 0%

profile of v1, /device:TPU:73, one launch (start us, length us, event | category | flops | bytes accessed | tf_op | source)
XLA Modules:
  0.0 306.8 jit_solution(4806732629466987560)
XLA Ops:
  5.1 3.2 %collective-permute-start.6 = (f32[5,4,48,1]{3,2,1,0:T(8,128)}, f32[5,4,48,1]{3,2,1,0:T(8,128)}, u32[]{:S(2)}, u32[]{:S(2)}) collective-permute-start(f32[5,4,48,1]{3,2,1,0:T(8,128)} %get-tuple-element.35), channel_id=1, source_target_pairs={{0,1},{1,2},{2,3},{3,4},{4,5},{5,6},{6,7},{7,8},{8,9},{9,10},{10,1... | collective-permute-start | bytes 11528 | tf_op jit(solution)/shard_map/ppermute | solution.py:22
  9.0 3.1 %collective-permute-start.5 = (f32[5,4,1,384]{3,2,1,0:T(1,128)}, f32[5,4,1,384]{3,2,1,0:T(1,128)}, u32[]{:S(2)}, u32[]{:S(2)}) collective-permute-start(f32[5,4,1,384]{3,2,1,0:T(1,128)} %get-tuple-element.32), channel_id=1, source_target_pairs={{16,0},{32,16},{48,32},{64,48},{80,64},{96,80},{112,96},{17,1},{33... | collective-permute-start | bytes 92168 | tf_op jit(solution)/shard_map/ppermute | solution.py:21
  12.1 3.0 collective-permute-start.4
  26.5 3.7 %multiply_add_fusion.3 = f32[5,4,48,384]{3,2,1,0:T(8,128)S(1)} fusion(f32[5,4,48,384]{3,2,1,0:T(8,128)S(1)} %copy-done, f32[5,4,48,1]{3,2,1,0:T(8,128)} %collective-permute-done.7, f32[5,4,48,383]{3,2,1,0:T(8,128)} %get-tuple-element.38, f32[5,4,48,383]{3,2,1,0:T(8,128)S(1)} %get-tuple-element.37, f32[5,4,48,1]{3,2,1,0:T(8,128)} %collective-permute-done.6, ...), kind=kLoop, calls=%fused_computation.35 | loop fusion | flops 8478720 | bytes 10321920 | tf_op jit(solution)/shard_map/add | solution.py:41
  30.2 2.9 pad_dynamic-slice_fusion.3
  33.2 3.3 %collective-permute-start.12 = (f32[5,4,48,130]{3,2,1,0:T(8,128)}, f32[5,4,48,130]{3,2,1,0:T(8,128)}, u32[]{:S(2)}, u32[]{:S(2)}) collective-permute-start(f32[5,4,48,130]{3,2,1,0:T(8,128)} %get-tuple-element.29), channel_id=1, source_target_pairs={{9,2},{10,5},{11,8},{12,11},{13,14},{25,18},{26,21},{27,24},{28,27... | collective-permute-start | bytes 1497608 | tf_op jit(solution)/shard_map/ppermute | solution.py:137
  51.9 26.2 %collective-permute-done.12 = f32[5,4,48,130]{3,2,1,0:T(8,128)} collective-permute-done((f32[5,4,48,130]{3,2,1,0:T(8,128)}, f32[5,4,48,130]{3,2,1,0:T(8,128)}, u32[]{:S(2)}, u32[]{:S(2)}) %collective-permute-start.12) | collective-permute-done | bytes 499232 | tf_op jit(solution)/shard_map/ppermute | solution.py:137
  78.0 28.6 %collective-permute-start.3 = (f32[5,4,48,1]{3,2,1,0:T(8,128)}, f32[5,4,48,1]{3,2,1,0:T(8,128)}, u32[]{:S(2)}, u32[]{:S(2)}) collective-permute-start(f32[5,4,48,1]{3,2,1,0:T(8,128)} %get-tuple-element.23), channel_id=1, source_target_pairs={{1,0},{2,1},{3,2},{4,3},{5,4},{6,5},{7,6},{8,7},{9,8},{10,9},{11,1... | collective-permute-start | bytes 11528 | tf_op jit(solution)/shard_map/ppermute | solution.py:23
  125.0 4.7 %all-to-all-start = ((f32[8,5,4,18,130]{4,2,3,1,0:T(4,128)}), f32[8,5,4,18,130]{4,2,3,1,0:T(4,128)}, u32[]{:S(2)}, u32[]{:S(2)}) async-start(f32[8,5,4,18,130]{4,2,3,1,0:T(4,128)} %bitcast_dynamic-update-slice_fusion), calls=%async_computation | async-start | bytes 5898240 | tf_op jit(solution)/shard_map/all_to_all | solution.py:146
  135.4 29.8 %all-to-all-done = f32[8,5,4,18,130]{4,2,3,1,0:T(4,128)} async-done(((f32[8,5,4,18,130]{4,2,3,1,0:T(4,128)}), f32[8,5,4,18,130]{4,2,3,1,0:T(4,128)}, u32[]{:S(2)}, u32[]{:S(2)}) %all-to-all-start) | async-done | bytes 1497632 | tf_op jit(solution)/shard_map/all_to_all | solution.py:146
  169.8 3.6 %copy.41 = f32[5,4,48,128,3]{2,1,4,3,0:T(4,128)} copy(f32[5,4,48,128,3]{3,1,2,0,4:T(4,128)S(1)} %pad_maximum_fusion.8) | data formatting | bytes 2949120 | tf_op jit(solution)/shard_map/stack | solution.py:59
  173.4 3.4 %copy.42 = f32[5,4,48,384]{3,2,1,0:T(8,128)S(1)} copy(f32[5,4,48,384]{2,1,3,0:T(4,128)} %bitcast.62) | data formatting | bytes 2949120 | tf_op jit(solution)/shard_map/reshape | solution.py:63
  176.8 4.1 %multiply_add_fusion.2 = f32[5,4,48,384]{3,2,1,0:T(8,128)S(1)} fusion(f32[5,4,48,384]{3,2,1,0:T(8,128)S(1)} %copy.42, f32[5,4,48,384]{3,2,1,0:T(8,128)S(1)} %copy-done.1, f32[5,4,48,1]{3,2,1,0:T(8,128)} %collective-permute-done.3, f32[5,4,48,383]{3,2,1,0:T(8,128)} %get-tuple-element.25, f32[5,4,48,383]{3,2,1,0:T(8,128)} %get-tuple-element.24, ...), kind=kLoop, calls=%fused_computation.34 | loop fusion | flops 9584640 | bytes 11870208 | tf_op jit(solution)/shard_map/add | solution.py:157
  181.7 3.6 %collective-permute-start.16 = (f32[5,4,48,1]{3,2,1,0:T(8,128)S(1)}, f32[5,4,48,1]{3,2,1,0:T(8,128)S(1)}, u32[]{:S(2)}, u32[]{:S(2)}) collective-permute-start(f32[5,4,48,1]{3,2,1,0:T(8,128)S(1)} %get-tuple-element.15), channel_id=1, source_target_pairs={{1,0},{2,1},{3,2},{4,3},{5,4},{6,5},{7,6},{8,7},{9,8},{10,9},{11,1... | collective-permute-start | bytes 11528 | tf_op jit(solution)/shard_map/ppermute | solution.py:23
  187.3 3.1 collective-permute-start.14
  195.5 4.7 %collective-permute-done.15 = f32[5,4,48,1]{3,2,1,0:T(8,128)S(1)} collective-permute-done((f32[5,4,48,1]{3,2,1,0:T(8,128)S(1)}, f32[5,4,48,1]{3,2,1,0:T(8,128)S(1)}, u32[]{:S(2)}, u32[]{:S(2)}) %collective-permute-start.15) | collective-permute-done | bytes 3872 | tf_op jit(solution)/shard_map/ppermute | solution.py:22
  202.7 5.2 %collective-permute-start.20 = (f32[5,4,48,1]{3,2,1,0:T(8,128)S(1)}, f32[5,4,48,1]{3,2,1,0:T(8,128)S(1)}, u32[]{:S(2)}, u32[]{:S(2)}) collective-permute-start(f32[5,4,48,1]{3,2,1,0:T(8,128)S(1)} %get-tuple-element.7), channel_id=1, source_target_pairs={{1,0},{2,1},{3,2},{4,3},{5,4},{6,5},{7,6},{8,7},{9,8},{10,9},{11,1... | collective-permute-start | bytes 11528 | tf_op jit(solution)/shard_map/ppermute | solution.py:23
  209.8 4.3 %collective-permute-start.18 = (f32[5,4,1,384]{3,2,1,0:T(1,128)S(1)}, f32[5,4,1,384]{3,2,1,0:T(1,128)S(1)}, u32[]{:S(2)}, u32[]{:S(2)}) collective-permute-start(f32[5,4,1,384]{3,2,1,0:T(1,128)S(1)} %get-tuple-element.3), channel_id=1, source_target_pairs={{16,0},{32,16},{48,32},{64,48},{80,64},{96,80},{112,96},{17,1},{33... | collective-permute-start | bytes 92168 | tf_op jit(solution)/shard_map/ppermute | solution.py:21
  216.5 3.7 %collective-permute-done.19 = f32[5,4,48,1]{3,2,1,0:T(8,128)S(1)} collective-permute-done((f32[5,4,48,1]{3,2,1,0:T(8,128)S(1)}, f32[5,4,48,1]{3,2,1,0:T(8,128)S(1)}, u32[]{:S(2)}, u32[]{:S(2)}) %collective-permute-start.19) | collective-permute-done | bytes 3872 | tf_op jit(solution)/shard_map/ppermute | solution.py:22
  223.1 3.5 %collective-permute-start.21 = (f32[5,4,16,128]{3,2,1,0:T(8,128)S(1)}, f32[5,4,16,128]{3,2,1,0:T(8,128)S(1)}, u32[]{:S(2)}, u32[]{:S(2)}) collective-permute-start(f32[5,4,16,128]{3,2,1,0:T(8,128)S(1)} %fusion), channel_id=1, source_target_pairs={{0,16},{16,32},{32,48},{48,64},{64,80},{80,96},{96,112},{112,0},{1... | collective-permute-start | bytes 491528 | tf_op jit(solution)/shard_map/ppermute | solution.py:164
  241.4 3.5 %collective-permute-start.27 = (f32[5,4,16,128]{3,2,1,0:T(8,128)S(1)}, f32[5,4,16,128]{3,2,1,0:T(8,128)S(1)}, u32[]{:S(2)}, u32[]{:S(2)}) collective-permute-start(f32[5,4,16,128]{3,2,1,0:T(8,128)S(1)} %collective-permute-done.26), channel_id=1, source_target_pairs={{0,112},{16,0},{32,16},{48,32},{64,48},{80,64},{96,80},{112,96},{1... | collective-permute-start | bytes 491528 | tf_op jit(solution)/shard_map/ppermute | solution.py:167
  249.7 6.2 %collective-permute-start.30 = (f32[5,4,48,128]{3,2,1,0:T(8,128)S(1)}, f32[5,4,48,128]{3,2,1,0:T(8,128)S(1)}, u32[]{:S(2)}, u32[]{:S(2)}) collective-permute-start(f32[5,4,48,128]{3,2,1,0:T(8,128)S(1)} %pad_dynamic-slice_fusion.13), channel_id=1, source_target_pairs={{0,8},{3,9},{6,10},{9,11},{12,12},{15,13},{16,24},{19,25},{22,26},... | collective-permute-start | bytes 1474568 | tf_op jit(solution)/shard_map/ppermute | solution.py:181
  259.2 33.2 %collective-permute-done.28 = f32[5,4,48,128]{3,2,1,0:T(8,128)S(1)} collective-permute-done((f32[5,4,48,128]{3,2,1,0:T(8,128)S(1)}, f32[5,4,48,128]{3,2,1,0:T(8,128)S(1)}, u32[]{:S(2)}, u32[]{:S(2)}) %collective-permute-start.28) | collective-permute-done | bytes 491552 | tf_op jit(solution)/shard_map/ppermute | solution.py:181
  292.6 12.5 %collective-permute-done.32 = f32[5,4,48,128]{3,2,1,0:T(8,128)S(1)} collective-permute-done((f32[5,4,48,128]{3,2,1,0:T(8,128)S(1)}, f32[5,4,48,128]{3,2,1,0:T(8,128)S(1)}, u32[]{:S(2)}, u32[]{:S(2)}) %collective-permute-start.32) | collective-permute-done | bytes 491552 | tf_op jit(solution)/shard_map/ppermute | solution.py:181
  (145 shorter events, 90.8 us)
Async XLA Ops:
  3.0 23.5 %collective-permute-start.7 = (f32[5,4,48,1]{3,2,1,0:T(8,128)}, f32[5,4,48,1]{3,2,1,0:T(8,128)}, u32[]{:S(2)}, u32[]{:S(2)}) collective-permute-start(f32[5,4,48,1]{3,2,1,0:T(8,128)} %get-tuple-element.36), channel_id=1, source_target_pairs={{1,0},{2,1},{3,2},{4,3},{5,4},{6,5},{7,6},{8,7},{9,8},{10,9},{11,1... | collective-permute-start | bytes 11528 | tf_op jit(solution)/shard_map/ppermute | solution.py:23
  5.1 21.4 %collective-permute-start.6 = (f32[5,4,48,1]{3,2,1,0:T(8,128)}, f32[5,4,48,1]{3,2,1,0:T(8,128)}, u32[]{:S(2)}, u32[]{:S(2)}) collective-permute-start(f32[5,4,48,1]{3,2,1,0:T(8,128)} %get-tuple-element.35), channel_id=1, source_target_pairs={{0,1},{1,2},{2,3},{3,4},{4,5},{5,6},{6,7},{7,8},{8,9},{9,10},{10,1... | collective-permute-start | bytes 11528 | tf_op jit(solution)/shard_map/ppermute | solution.py:22
  9.0 17.5 %collective-permute-start.5 = (f32[5,4,1,384]{3,2,1,0:T(1,128)}, f32[5,4,1,384]{3,2,1,0:T(1,128)}, u32[]{:S(2)}, u32[]{:S(2)}) collective-permute-start(f32[5,4,1,384]{3,2,1,0:T(1,128)} %get-tuple-element.32), channel_id=1, source_target_pairs={{16,0},{32,16},{48,32},{64,48},{80,64},{96,80},{112,96},{17,1},{33... | collective-permute-start | bytes 92168 | tf_op jit(solution)/shard_map/ppermute | solution.py:21
  12.1 14.4 %collective-permute-start.4 = (f32[5,4,1,384]{3,2,1,0:T(1,128)}, f32[5,4,1,384]{3,2,1,0:T(1,128)}, u32[]{:S(2)}, u32[]{:S(2)}) collective-permute-start(f32[5,4,1,384]{3,2,1,0:T(1,128)} %get-tuple-element.31), channel_id=1, source_target_pairs={{0,16},{16,32},{32,48},{48,64},{64,80},{80,96},{96,112},{1,17},{17... | collective-permute-start | bytes 92168 | tf_op jit(solution)/shard_map/ppermute | solution.py:20
  33.2 44.8 %collective-permute-start.12 = (f32[5,4,48,130]{3,2,1,0:T(8,128)}, f32[5,4,48,130]{3,2,1,0:T(8,128)}, u32[]{:S(2)}, u32[]{:S(2)}) collective-permute-start(f32[5,4,48,130]{3,2,1,0:T(8,128)} %get-tuple-element.29), channel_id=1, source_target_pairs={{9,2},{10,5},{11,8},{12,11},{13,14},{25,18},{26,21},{27,24},{28,27... | collective-permute-start | bytes 1497608 | tf_op jit(solution)/shard_map/ppermute | solution.py:137
  36.5 70.1 %collective-permute-start.11 = (f32[5,4,48,130]{3,2,1,0:T(8,128)}, f32[5,4,48,130]{3,2,1,0:T(8,128)}, u32[]{:S(2)}, u32[]{:S(2)}) collective-permute-start(f32[5,4,48,130]{3,2,1,0:T(8,128)} %get-tuple-element.28), channel_id=1, source_target_pairs={{8,2},{9,5},{10,8},{11,11},{12,14},{24,18},{25,21},{26,24},{27,27}... | collective-permute-start | bytes 1497608 | tf_op jit(solution)/shard_map/ppermute | solution.py:137
  38.7 69.8 %collective-permute-start.10 = (f32[5,4,48,130]{3,2,1,0:T(8,128)}, f32[5,4,48,130]{3,2,1,0:T(8,128)}, u32[]{:S(2)}, u32[]{:S(2)}) collective-permute-start(f32[5,4,48,130]{3,2,1,0:T(8,128)} %get-tuple-element.27), channel_id=1, source_target_pairs={{9,1},{10,4},{11,7},{12,10},{13,13},{25,17},{26,20},{27,23},{28,26... | collective-permute-start | bytes 1497608 | tf_op jit(solution)/shard_map/ppermute | solution.py:137
  41.0 70.3 %collective-permute-start.8 = (f32[5,4,48,130]{3,2,1,0:T(8,128)S(1)}, f32[5,4,48,130]{3,2,1,0:T(8,128)}, u32[]{:S(2)}, u32[]{:S(2)}) collective-permute-start(f32[5,4,48,130]{3,2,1,0:T(8,128)S(1)} %get-tuple-element.30), channel_id=1, source_target_pairs={{8,0},{9,3},{10,6},{11,9},{12,12},{13,15},{24,16},{25,19},{26,22},... | collective-permute-start | bytes 1497608 | tf_op jit(solution)/shard_map/ppermute | solution.py:137
  43.2 70.9 %collective-permute-start.9 = (f32[5,4,48,130]{3,2,1,0:T(8,128)S(1)}, f32[5,4,48,130]{3,2,1,0:T(8,128)}, u32[]{:S(2)}, u32[]{:S(2)}) collective-permute-start(f32[5,4,48,130]{3,2,1,0:T(8,128)S(1)} %get-tuple-element.26), channel_id=1, source_target_pairs={{8,1},{9,4},{10,7},{11,10},{12,13},{24,17},{25,20},{26,23},{27,26}... | collective-permute-start | bytes 1497608 | tf_op jit(solution)/shard_map/ppermute | solution.py:137
  78.0 98.8 %collective-permute-start.3 = (f32[5,4,48,1]{3,2,1,0:T(8,128)}, f32[5,4,48,1]{3,2,1,0:T(8,128)}, u32[]{:S(2)}, u32[]{:S(2)}) collective-permute-start(f32[5,4,48,1]{3,2,1,0:T(8,128)} %get-tuple-element.23), channel_id=1, source_target_pairs={{1,0},{2,1},{3,2},{4,3},{5,4},{6,5},{7,6},{8,7},{9,8},{10,9},{11,1... | collective-permute-start | bytes 11528 | tf_op jit(solution)/shard_map/ppermute | solution.py:23
  106.6 70.2 %collective-permute-start.2 = (f32[5,4,48,1]{3,2,1,0:T(8,128)}, f32[5,4,48,1]{3,2,1,0:T(8,128)}, u32[]{:S(2)}, u32[]{:S(2)}) collective-permute-start(f32[5,4,48,1]{3,2,1,0:T(8,128)} %get-tuple-element.22), channel_id=1, source_target_pairs={{0,1},{1,2},{2,3},{3,4},{4,5},{5,6},{6,7},{7,8},{8,9},{9,10},{10,1... | collective-permute-start | bytes 11528 | tf_op jit(solution)/shard_map/ppermute | solution.py:22
  108.5 68.3 %collective-permute-start.1 = (f32[5,4,1,384]{3,2,1,0:T(1,128)}, f32[5,4,1,384]{3,2,1,0:T(1,128)}, u32[]{:S(2)}, u32[]{:S(2)}) collective-permute-start(f32[5,4,1,384]{3,2,1,0:T(1,128)} %get-tuple-element.19), channel_id=1, source_target_pairs={{16,0},{32,16},{48,32},{64,48},{80,64},{96,80},{112,96},{17,1},{33... | collective-permute-start | bytes 92168 | tf_op jit(solution)/shard_map/ppermute | solution.py:21
  111.3 65.5 %collective-permute-start = (f32[5,4,1,384]{3,2,1,0:T(1,128)}, f32[5,4,1,384]{3,2,1,0:T(1,128)}, u32[]{:S(2)}, u32[]{:S(2)}) collective-permute-start(f32[5,4,1,384]{3,2,1,0:T(1,128)} %get-tuple-element.18), channel_id=1, source_target_pairs={{0,16},{16,32},{32,48},{48,64},{64,80},{80,96},{96,112},{1,17},{17... | collective-permute-start | bytes 92168 | tf_op jit(solution)/shard_map/ppermute | solution.py:20
  125.0 40.2 %all-to-all-start = ((f32[8,5,4,18,130]{4,2,3,1,0:T(4,128)}), f32[8,5,4,18,130]{4,2,3,1,0:T(4,128)}, u32[]{:S(2)}, u32[]{:S(2)}) async-start(f32[8,5,4,18,130]{4,2,3,1,0:T(4,128)} %bitcast_dynamic-update-slice_fusion), calls=%async_computation | async-start | bytes 5898240 | tf_op jit(solution)/shard_map/all_to_all | solution.py:146
  181.7 13.8 %collective-permute-start.16 = (f32[5,4,48,1]{3,2,1,0:T(8,128)S(1)}, f32[5,4,48,1]{3,2,1,0:T(8,128)S(1)}, u32[]{:S(2)}, u32[]{:S(2)}) collective-permute-start(f32[5,4,48,1]{3,2,1,0:T(8,128)S(1)} %get-tuple-element.15), channel_id=1, source_target_pairs={{1,0},{2,1},{3,2},{4,3},{5,4},{6,5},{7,6},{8,7},{9,8},{10,9},{11,1... | collective-permute-start | bytes 11528 | tf_op jit(solution)/shard_map/ppermute | solution.py:23
  185.4 14.8 %collective-permute-start.15 = (f32[5,4,48,1]{3,2,1,0:T(8,128)S(1)}, f32[5,4,48,1]{3,2,1,0:T(8,128)S(1)}, u32[]{:S(2)}, u32[]{:S(2)}) collective-permute-start(f32[5,4,48,1]{3,2,1,0:T(8,128)S(1)} %get-tuple-element.14), channel_id=1, source_target_pairs={{0,1},{1,2},{2,3},{3,4},{4,5},{5,6},{6,7},{7,8},{8,9},{9,10},{10,1... | collective-permute-start | bytes 11528 | tf_op jit(solution)/shard_map/ppermute | solution.py:22
  187.3 12.9 %collective-permute-start.14 = (f32[5,4,1,384]{3,2,1,0:T(1,128)S(1)}, f32[5,4,1,384]{3,2,1,0:T(1,128)S(1)}, u32[]{:S(2)}, u32[]{:S(2)}) collective-permute-start(f32[5,4,1,384]{3,2,1,0:T(1,128)S(1)} %get-tuple-element.11), channel_id=1, source_target_pairs={{16,0},{32,16},{48,32},{64,48},{80,64},{96,80},{112,96},{17,1},{33... | collective-permute-start | bytes 92168 | tf_op jit(solution)/shard_map/ppermute | solution.py:21
  202.7 13.7 %collective-permute-start.20 = (f32[5,4,48,1]{3,2,1,0:T(8,128)S(1)}, f32[5,4,48,1]{3,2,1,0:T(8,128)S(1)}, u32[]{:S(2)}, u32[]{:S(2)}) collective-permute-start(f32[5,4,48,1]{3,2,1,0:T(8,128)S(1)} %get-tuple-element.7), channel_id=1, source_target_pairs={{1,0},{2,1},{3,2},{4,3},{5,4},{6,5},{7,6},{8,7},{9,8},{10,9},{11,1... | collective-permute-start | bytes 11528 | tf_op jit(solution)/shard_map/ppermute | solution.py:23
  207.9 12.3 %collective-permute-start.19 = (f32[5,4,48,1]{3,2,1,0:T(8,128)S(1)}, f32[5,4,48,1]{3,2,1,0:T(8,128)S(1)}, u32[]{:S(2)}, u32[]{:S(2)}) collective-permute-start(f32[5,4,48,1]{3,2,1,0:T(8,128)S(1)} %get-tuple-element.6), channel_id=1, source_target_pairs={{0,1},{1,2},{2,3},{3,4},{4,5},{5,6},{6,7},{7,8},{8,9},{9,10},{10,1... | collective-permute-start | bytes 11528 | tf_op jit(solution)/shard_map/ppermute | solution.py:22
  246.5 45.9 %collective-permute-start.28 = (f32[5,4,48,128]{3,2,1,0:T(8,128)S(1)}, f32[5,4,48,128]{3,2,1,0:T(8,128)S(1)}, u32[]{:S(2)}, u32[]{:S(2)}) collective-permute-start(f32[5,4,48,128]{3,2,1,0:T(8,128)S(1)} %pad_dynamic-slice_fusion.13), channel_id=1, source_target_pairs={{1,9},{4,10},{7,11},{10,12},{13,13},{17,25},{20,26},{23,27},{26,28... | collective-permute-start | bytes 1474568 | tf_op jit(solution)/shard_map/ppermute | solution.py:181
  247.8 44.7 %collective-permute-start.29 = (f32[5,4,48,128]{3,2,1,0:T(8,128)S(1)}, f32[5,4,48,128]{3,2,1,0:T(8,128)S(1)}, u32[]{:S(2)}, u32[]{:S(2)}) collective-permute-start(f32[5,4,48,128]{3,2,1,0:T(8,128)S(1)} %pad_dynamic-slice_fusion.13), channel_id=1, source_target_pairs={{2,9},{5,10},{8,11},{11,12},{14,13},{18,25},{21,26},{24,27},{27,28... | collective-permute-start | bytes 1474568 | tf_op jit(solution)/shard_map/ppermute | solution.py:181
  249.7 42.8 %collective-permute-start.30 = (f32[5,4,48,128]{3,2,1,0:T(8,128)S(1)}, f32[5,4,48,128]{3,2,1,0:T(8,128)S(1)}, u32[]{:S(2)}, u32[]{:S(2)}) collective-permute-start(f32[5,4,48,128]{3,2,1,0:T(8,128)S(1)} %pad_dynamic-slice_fusion.13), channel_id=1, source_target_pairs={{0,8},{3,9},{6,10},{9,11},{12,12},{15,13},{16,24},{19,25},{22,26},... | collective-permute-start | bytes 1474568 | tf_op jit(solution)/shard_map/ppermute | solution.py:181
  256.6 36.0 %collective-permute-start.31 = (f32[5,4,48,128]{3,2,1,0:T(8,128)S(1)}, f32[5,4,48,128]{3,2,1,0:T(8,128)S(1)}, u32[]{:S(2)}, u32[]{:S(2)}) collective-permute-start(f32[5,4,48,128]{3,2,1,0:T(8,128)S(1)} %pad_dynamic-slice_fusion.13), channel_id=1, source_target_pairs={{1,8},{4,9},{7,10},{10,11},{13,12},{17,24},{20,25},{23,26},{26,27}... | collective-permute-start | bytes 1474568 | tf_op jit(solution)/shard_map/ppermute | solution.py:181
  257.9 47.2 %collective-permute-start.32 = (f32[5,4,48,128]{3,2,1,0:T(8,128)S(1)}, f32[5,4,48,128]{3,2,1,0:T(8,128)S(1)}, u32[]{:S(2)}, u32[]{:S(2)}) collective-permute-start(f32[5,4,48,128]{3,2,1,0:T(8,128)S(1)} %pad_dynamic-slice_fusion.13), channel_id=1, source_target_pairs={{2,8},{5,9},{8,10},{11,11},{14,12},{18,24},{21,25},{24,26},{27,27}... | collective-permute-start | bytes 1474568 | tf_op jit(solution)/shard_map/ppermute | solution.py:181
  (22 other events, 176.9 us)
